TPU v7x, 32 devices: a whole 2x2x4 slice. The times are simulated.
32 devices in a mesh: elem: 8 (over z, x), span: 4 (over y, core).
Axes of the slice: x: 2, y: 2, z: 4, core: 2. Of those that a mesh axis runs over, the one named last changes fastest.
Arguments:
- column_state: bfloat16 [24576, 1152], P(('elem', 'span')), may hold values from -6 to 6
- counts: int32 [32], replicated, may hold values from 128 to 768, as said below
- edge_index: int32 [32, 4, 16], P(('elem', 'span')), may hold values from 0 to 127, as said below
- encode_first: bfloat16 [3, 32, 16], replicated, may hold values from -0.875 to 0.875
- encode_second: bfloat16 [8, 3, 32, 32], replicated, may hold values from -0.625 to 0.625
- middle_first: bfloat16 [3, 64, 32], replicated, may hold values from -0.625 to 0.625
- middle_second: bfloat16 [8, 3, 64, 64], replicated, may hold values from -0.4375 to 0.4375
- decode_first: bfloat16 [3, 32, 96], replicated, may hold values from -0.375 to 0.375
- decode_second: bfloat16 [8, 3, 32, 32], replicated, may hold values from -0.625 to 0.625
- output_weight: bfloat16 [3, 16, 32], replicated, may hold values from -0.625 to 0.625
Outputs:
- tendencies: bfloat16 [24576, 1152], P(('elem', 'span'))
Inputs may be any that keep to these rules, and one draw needn't show every extreme that they name: counts sum to 8192. `edge_index`: the 64 entries of one owner are distinct.
All inputs are finite; a program needn't handle non-finite values.
Results may differ from a plain program's by a relative error of at most 0.0085.
Values may be sent and summed in bfloat16 or wider, within the bound.
A program may use at most 64 MiB of HBM per device.

v0:
```python
import math
import jax
import jax.numpy as jnp
from jax import lax
from jax.sharding import PartitionSpec as P

LEV = 72
F_IN = 16
F_OUT = 16
DEPTH = 8
SPAN = 256


def extended(cells, sides, width):
    for axis, dim in sides:
        count = lax.axis_size(axis)
        head = lax.slice_in_dim(cells, 0, width, axis=dim)
        tail = lax.slice_in_dim(cells, cells.shape[dim] - width, cells.shape[dim], axis=dim)
        cells = jnp.concatenate(
            [
                lax.ppermute(tail, axis, [(i, (i + 1) % count) for i in range(count)]),
                cells,
                lax.ppermute(head, axis, [((i + 1) % count, i) for i in range(count)]),
            ],
            axis=dim,
        )
    return cells


def conv_levels(profile, weight):
    levels = profile.shape[1]
    padded = jnp.pad(profile, ((0, 0), (1, 1), (0, 0)))
    stacked = jnp.concatenate(
        [padded[:, tap_index : tap_index + levels, :] for tap_index in range(3)], axis=0
    )
    flat_weight = weight.transpose(1, 0, 2).reshape(weight.shape[1], 3 * weight.shape[2])
    return jnp.einsum("ok,kln->oln", flat_weight, stacked, preferred_element_type=jnp.float32)


def residual_stack(hidden, stacked_weights):
    for layer_index in range(DEPTH):
        update = jax.nn.silu(conv_levels(hidden, stacked_weights[layer_index]))
        hidden = (hidden.astype(jnp.float32) + update).astype(jnp.bfloat16)
    return hidden


def network(columns, weights):
    (
        encode_first,
        encode_second,
        middle_first,
        middle_second,
        decode_first,
        decode_second,
        output_weight,
    ) = weights
    inputs = columns.reshape(columns.shape[0], F_IN, LEV).transpose(1, 2, 0)
    hidden = jax.nn.silu(conv_levels(inputs, encode_first)).astype(jnp.bfloat16)
    skipped = residual_stack(hidden, encode_second)
    pooled = (
        0.5 * (skipped[:, 0::2].astype(jnp.float32) + skipped[:, 1::2].astype(jnp.float32))
    ).astype(jnp.bfloat16)
    middle = jax.nn.silu(conv_levels(pooled, middle_first)).astype(jnp.bfloat16)
    middle = residual_stack(middle, middle_second)
    raised = jnp.repeat(middle, 2, axis=1)
    joined = jnp.concatenate([raised, skipped], axis=0)
    decoded = jax.nn.silu(conv_levels(joined, decode_first)).astype(jnp.bfloat16)
    decoded = residual_stack(decoded, decode_second)
    result = conv_levels(decoded, output_weight).astype(jnp.bfloat16)
    return result.transpose(2, 0, 1).reshape(columns.shape[0], F_OUT * LEV)


def on_device(
    column_state,
    counts,
    edge_index,
    encode_first,
    encode_second,
    middle_first,
    middle_second,
    decode_first,
    decode_second,
    output_weight,
):
    weights = (
        encode_first,
        encode_second,
        middle_first,
        middle_second,
        decode_first,
        decode_second,
        output_weight,
    )
    devices = lax.axis_size(("elem", "span"))
    device_index = lax.axis_index(("elem", "span"))
    col_max = column_state.shape[0]
    feat_in = column_state.shape[1]
    feat_out = F_OUT * LEV
    slot_count = col_max // devices
    offsets = jnp.concatenate([jnp.zeros((1,), jnp.int32), jnp.cumsum(counts)])
    rank_start = offsets[device_index]
    slot_grid = column_state.reshape(slot_count, devices, feat_in)
    outgoing = jnp.roll(slot_grid, rank_start, axis=1)
    arrived = lax.all_to_all(outgoing, ("elem", "span"), split_axis=1, concat_axis=1, tiled=True)
    block_ranks = jnp.arange(SPAN, dtype=jnp.int32) * devices + device_index
    source = jnp.sum((offsets[None, 1:] <= block_ranks[:, None]).astype(jnp.int32), axis=1)
    within = block_ranks - offsets[source]
    flat_index = within // devices * devices + source
    dense_rows = arrived.reshape(slot_count * devices, feat_in)[flat_index]
    block_rows = math.gcd(SPAN, 128)
    computed = lax.map(
        lambda rows_block: network(rows_block, weights), dense_rows.reshape(-1, block_rows, feat_in)
    )
    computed = computed.reshape(SPAN, feat_out)
    slot_back = (
        jnp.zeros((slot_count * devices, feat_out), jnp.bfloat16).at[flat_index].set(computed)
    )
    slot_back = slot_back.reshape(slot_count, devices, feat_out)
    returned = lax.all_to_all(slot_back, ("elem", "span"), split_axis=1, concat_axis=1, tiled=True)
    owned = jnp.roll(returned, -rank_start, axis=1).reshape(col_max, feat_out)
    edge_local = edge_index[0]
    edge_rows = owned[edge_local]
    across = extended(edge_rows[0:2], (("elem", 0),), 1)
    upward = extended(edge_rows[2:4], (("span", 0),), 1)
    edge_float = edge_rows.astype(jnp.float32)
    west_edge = 0.5 * (edge_float[0] + across[0].astype(jnp.float32))
    east_edge = 0.5 * (edge_float[1] + across[3].astype(jnp.float32))
    south_edge = 0.5 * (edge_float[2] + upward[0].astype(jnp.float32))
    north_edge = 0.5 * (edge_float[3] + upward[3].astype(jnp.float32))
    merged = jnp.stack([west_edge, east_edge, south_edge, north_edge], axis=0).astype(jnp.bfloat16)
    owned = owned.at[edge_local.reshape(-1)].set(merged.reshape(-1, feat_out))
    return owned


def solution(mesh):
    return jax.shard_map(
        on_device,
        mesh=mesh,
        in_specs=(
            P(("elem", "span"), None),
            P(),
            P(("elem", "span"), None, None),
            P(),
            P(),
            P(),
            P(),
            P(),
            P(),
            P(),
        ),
        out_specs=P(("elem", "span"), None),
        check_vma=False,
    )
```

profile of v0, /device:TPU:0, one launch (start us, length us, event | category | flops | bytes accessed | tf_op | source)
XLA Modules:
  0.0 176.2 jit_solution(497506823206754736)
XLA Ops:
  0.0 0.7 copy.116
  1.0 0.6 dynamic_slice.13
  3.5 2.8 %fusion.332 = bf16[24,32,1152]{2,1,0:T(8,128)(2,1)S(1)} fusion(s32[]{:T(128)S(6)} %select_n.75, bf16[24,32,1152]{2,1,0:T(8,128)(2,1)} %bitcast.526), kind=kLoop, calls=%fused_computation.341 | loop fusion | flops 3538944 | bytes 3538948 | tf_op jit(solution)/shard_map/jit(_roll_dynamic)/concatenate | solution.py:103
  6.2 1.7 copy.117
  8.0 7.6 %all-to-all-start = ((bf16[24,32,1152]{2,0,1:T(8,128)(2,1)}), bf16[24,32,1152]{2,0,1:T(8,128)(2,1)}, u32[]{:S(2)}, u32[]{:S(2)}) async-start(bf16[24,32,1152]{2,0,1:T(8,128)(2,1)} %copy.117), calls=%async_computation | async-start | bytes 3538944 | tf_op jit(solution)/shard_map/all_to_all | solution.py:104
  16.2 0.6 fusion.351
  16.8 0.7 fusion.350
  17.6 3.6 %compare_select_fusion.3 = (s32[256,1]{0,1:T(1,128)S(1)}, s32[256,1]{0,1:T(1,128)S(1)}) fusion(s32[]{:T(128)} %bitcast.132, s32[]{:T(128)} %bitcast.133, s32[]{:T(128)} %bitcast.134, s32[]{:T(128)} %bitcast.135, s32[]{:T(128)} %bitcast.136, s32[]{:T(128)} %bitcast.137, s32[256,1]{0,1:T(1,128)S(1)} %bitcast.538), kind=kLoop, calls=%fused_computation.397 | loop fusion | flops 3840 | bytes 3096 | tf_op jit(solution)/shard_map/gather | solution.py:107
  21.3 16.4 %select_select_fusion = s32[256]{0:T(256)S(1)} fusion(pred[256]{0:T(512)(128)(4,1)S(1)} %get-tuple-element.217, pred[256]{0:T(512)(128)(4,1)S(1)} %get-tuple-element.216, pred[256]{0:T(512)(128)(4,1)S(1)} %get-tuple-element.215, pred[256]{0:T(512)(128)(4,1)S(1)} %get-tuple-element.214, pred[256]{0:T(512)(128)(4,1)S(1)} %get-tuple-element.213, ...), kind=kLoop, calls=%fused_computation.408 | loop fusion | flops 6656 | bytes 8808 | tf_op jit(solution)/shard_map/gather | solution.py:107
  37.7 19.6 %all-to-all-done = bf16[24,32,1152]{2,0,1:T(8,128)(2,1)} async-done(((bf16[24,32,1152]{2,0,1:T(8,128)(2,1)}), bf16[24,32,1152]{2,0,1:T(8,128)(2,1)}, u32[]{:S(2)}, u32[]{:S(2)}) %all-to-all-start) | async-done | bytes 1769504 | tf_op jit(solution)/shard_map/all_to_all | solution.py:104
  57.3 1.7 copy.118
  59.0 1.3 gather_fusion
  60.3 53.1 %while.12 = (s32[]{:T(128)}, bf16[2,128,1152]{2,1,0:T(8,128)(2,1)}, bf16[2,128,1152]{2,1,0:T(8,128)(2,1)S(1)}, bf16[3,32,16]{1,2,0:T(8,128)(2,1)S(1)}, bf16[8,3,...) while((s32[]{:T(128)}, bf16[2,128,1152]{2,1,0:T(8,128)(2,1)}, ...), condition=%wide.region_3.5_spmd, body=%wide.region_2.4_spmd.sunk | while | flops 2317344768 | bytes 136280240 | solution.py:111
  62.7 0.5 multiply_convert_fusion.8
  68.8 0.5 multiply_convert_fusion.10
  69.6 0.6 add_convert_fusion.56
  70.6 0.6 add_convert_fusion.57
  71.5 0.6 add_convert_fusion.58
  72.5 0.6 add_convert_fusion.59
  73.5 0.6 add_convert_fusion.60
  74.4 0.6 add_convert_fusion.61
  75.4 0.6 add_convert_fusion.62
  76.3 0.6 add_convert_fusion.63
  77.4 0.6 fusion.498
  78.0 1.6 multiply_convert_fusion.11
  86.1 0.8 copy-done.9
  95.2 0.5 multiply_convert_fusion.10
  96.1 0.6 add_convert_fusion.56
  97.0 0.6 add_convert_fusion.57
  98.0 0.6 add_convert_fusion.58
  99.0 0.6 add_convert_fusion.59
  99.9 0.6 add_convert_fusion.60
  100.9 0.6 add_convert_fusion.61
  101.8 0.6 add_convert_fusion.62
  102.8 0.6 add_convert_fusion.63
  103.9 0.6 fusion.498
  104.5 1.6 multiply_convert_fusion.11
  112.6 0.8 copy-done.9
  113.4 2.7 %scatter_custom_fusion = bf16[768,1152]{1,0:T(8,128)(2,1)S(1)} fusion(s32[256]{0:T(256)} %bitcast.541, bf16[256,1152]{1,0:T(8,128)(2,1)} %bitcast.545, bf16[]{:T(256)} %constant.112.clone.1), kind=kCustom, calls=%fused_computation.342 | custom fusion | bytes 1769984 | tf_op jit(solution)/shard_map/scatter | solution.py:116
  116.2 1.7 copy.126
  117.9 3.8 %all-to-all-start.1 = ((bf16[24,32,1152]{2,0,1:T(8,128)(2,1)}), bf16[24,32,1152]{2,0,1:T(8,128)(2,1)S(1)}, u32[]{:S(2)}, u32[]{:S(2)}) async-start(bf16[24,32,1152]{2,0,1:T(8,128)(2,1)} %copy.126), calls=%async_computation.1 | async-start | bytes 3538944 | tf_op jit(solution)/shard_map/all_to_all | solution.py:119
  122.6 40.9 %all-to-all-done.1 = bf16[24,32,1152]{2,0,1:T(8,128)(2,1)S(1)} async-done(((bf16[24,32,1152]{2,0,1:T(8,128)(2,1)}), bf16[24,32,1152]{2,0,1:T(8,128)(2,1)S(1)}, u32[]{:S(2)}, u32[]{:S(2)}) %all-to-all-start.1) | async-done | bytes 1769504 | tf_op jit(solution)/shard_map/all_to_all | solution.py:119
  163.5 0.7 fusion.331
  164.4 0.7 gather_fusion.1
  165.2 1.5 collective-permute-start
  167.2 3.3 %collective-permute-start.1 = (bf16[1,16,1152]{2,1,0:T(8,128)(2,1)S(1)}, bf16[1,16,1152]{2,1,0:T(8,128)(2,1)S(1)}, u32[]{:S(2)}, u32[]{:S(2)}) collective-permute-start(bf16[1,16,1152]{2,1,0:T(8,128)(2,1)S(1)} %get-tuple-element.335), channel_id=1, source_target_pairs={{4,0},{8,4},{12,8},{16,12},{20,16},{24,20},{28,24},{0,28},{5,1},{9... | collective-permute-start | bytes 110600 | tf_op jit(solution)/shard_map/ppermute | solution.py:23
  170.5 1.4 collective-permute-done
  172.4 3.9 %scatter_fusion = bf16[768,1152]{1,0:T(8,128)(2,1)} fusion(bf16[768,1152]{1,0:T(8,128)(2,1)} %bitcast.523, s32[64]{0:T(128)S(1)} %fusion.347, bf16[64,1152]{1,0:T(8,128)(2,1)S(1)} %bitcast.537), kind=kCustom, calls=%fused_computation.3 | custom fusion | bytes 442624 | tf_op jit(solution)/shard_map/scatter | solution.py:131
  (202 shorter events, 36.6 us)
Async XLA Ops:
  8.0 7.6 %copy-start.5 = (bf16[3,16,32]{2,1,0:T(8,128)(2,1)S(1)}, bf16[3,16,32]{2,1,0:T(8,128)(2,1)}, u32[]{:S(2)}) copy-start(bf16[3,16,32]{2,1,0:T(8,128)(2,1)} %param.23) | copy-start | bytes 9220
  8.0 7.6 %copy-start.4 = (bf16[3,32,96]{2,1,0:T(8,128)(2,1)S(1)}, bf16[3,32,96]{2,1,0:T(8,128)(2,1)}, u32[]{:S(2)}) copy-start(bf16[3,32,96]{2,1,0:T(8,128)(2,1)} %param.21) | copy-start | bytes 55300
  8.0 7.7 %copy-start.2 = (bf16[8,3,32,32]{3,2,1,0:T(8,128)(2,1)S(1)}, bf16[8,3,32,32]{3,2,1,0:T(8,128)(2,1)}, u32[]{:S(2)}) copy-start(bf16[8,3,32,32]{3,2,1,0:T(8,128)(2,1)} %param.18) | copy-start | bytes 147460
  8.0 7.8 %copy-start.3 = (bf16[8,3,32,32]{3,2,1,0:T(8,128)(2,1)S(1)}, bf16[8,3,32,32]{3,2,1,0:T(8,128)(2,1)}, u32[]{:S(2)}) copy-start(bf16[8,3,32,32]{3,2,1,0:T(8,128)(2,1)} %param.22) | copy-start | bytes 147460
  8.0 8.0 %copy-start.1 = (bf16[8,3,64,64]{3,2,1,0:T(8,128)(2,1)S(1)}, bf16[8,3,64,64]{3,2,1,0:T(8,128)(2,1)}, u32[]{:S(2)}) copy-start(bf16[8,3,64,64]{3,2,1,0:T(8,128)(2,1)} %param.20) | copy-start | bytes 589828
  8.0 49.3 %all-to-all-start = ((bf16[24,32,1152]{2,0,1:T(8,128)(2,1)}), bf16[24,32,1152]{2,0,1:T(8,128)(2,1)}, u32[]{:S(2)}, u32[]{:S(2)}) async-start(bf16[24,32,1152]{2,0,1:T(8,128)(2,1)} %copy.117), calls=%async_computation | async-start | bytes 3538944 | tf_op jit(solution)/shard_map/all_to_all | solution.py:104
  37.7 21.3 %copy-start.7 = (s32[256,1]{0,1:T(1,128)}, s32[256,1]{0,1:T(1,128)S(1)}, u32[]{:S(2)}) copy-start(s32[256,1]{0,1:T(1,128)S(1)} %compare_select_fusion) | copy-start | bytes 3076
  59.0 1.3 copy-start.10
  59.0 1.3 copy-start.11
  85.0 1.1 copy-start.8
  86.1 0.8 copy-start.9
  111.5 1.1 copy-start.8
  112.6 0.8 copy-start.9
  117.9 4.5 %copy-start.6 = (s32[1,4,16]{2,1,0:T(4,128)S(1)}, s32[1,4,16]{2,1,0:T(4,128)}, u32[]{:S(2)}) copy-start(s32[1,4,16]{2,1,0:T(4,128)} %param.16) | copy-start | bytes 772
  117.9 45.6 %all-to-all-start.1 = ((bf16[24,32,1152]{2,0,1:T(8,128)(2,1)}), bf16[24,32,1152]{2,0,1:T(8,128)(2,1)S(1)}, u32[]{:S(2)}, u32[]{:S(2)}) async-start(bf16[24,32,1152]{2,0,1:T(8,128)(2,1)} %copy.126), calls=%async_computation.1 | async-start | bytes 3538944 | tf_op jit(solution)/shard_map/all_to_all | solution.py:119
  164.4 7.9 %copy-start = (bf16[24,32,1152]{2,1,0:T(8,128)(2,1)}, bf16[24,32,1152]{2,1,0:T(8,128)(2,1)S(1)}, u32[]{:S(2)}) copy-start(bf16[24,32,1152]{2,1,0:T(8,128)(2,1)S(1)} %copy.127) | copy-start | bytes 5308420
  165.2 6.7 %collective-permute-start = (bf16[1,16,1152]{2,1,0:T(8,128)(2,1)S(1)}, bf16[1,16,1152]{2,1,0:T(8,128)(2,1)S(1)}, u32[]{:S(2)}, u32[]{:S(2)}) collective-permute-start(bf16[1,16,1152]{2,1,0:T(8,128)(2,1)S(1)} %get-tuple-element.332), channel_id=1, source_target_pairs={{0,4},{4,8},{8,12},{12,16},{16,20},{20,24},{24,28},{28,0},{1,5},{5... | collective-permute-start | bytes 110600 | tf_op jit(solution)/shard_map/ppermute | solution.py:21
  166.7 5.3 %collective-permute-start.3 = (bf16[1,16,1152]{2,1,0:T(8,128)(2,1)S(1)}, bf16[1,16,1152]{2,1,0:T(8,128)(2,1)S(1)}, u32[]{:S(2)}, u32[]{:S(2)}) collective-permute-start(bf16[1,16,1152]{2,1,0:T(8,128)(2,1)S(1)} %get-tuple-element.333), channel_id=1, source_target_pairs={{1,0},{2,1},{3,2},{0,3},{5,4},{6,5},{7,6},{4,7},{9,8},{10,9},{11,1... | collective-permute-start | bytes 110600 | tf_op jit(solution)/shard_map/ppermute | solution.py:23
  167.2 4.8 %collective-permute-start.2 = (bf16[1,16,1152]{2,1,0:T(8,128)(2,1)S(1)}, bf16[1,16,1152]{2,1,0:T(8,128)(2,1)S(1)}, u32[]{:S(2)}, u32[]{:S(2)}) collective-permute-start(bf16[1,16,1152]{2,1,0:T(8,128)(2,1)S(1)} %get-tuple-element.334), channel_id=1, source_target_pairs={{0,1},{1,2},{2,3},{3,0},{4,5},{5,6},{6,7},{7,4},{8,9},{9,10},{10,1... | collective-permute-start | bytes 110600 | tf_op jit(solution)/shard_map/ppermute | solution.py:21
  167.2 5.1 %collective-permute-start.1 = (bf16[1,16,1152]{2,1,0:T(8,128)(2,1)S(1)}, bf16[1,16,1152]{2,1,0:T(8,128)(2,1)S(1)}, u32[]{:S(2)}, u32[]{:S(2)}) collective-permute-start(bf16[1,16,1152]{2,1,0:T(8,128)(2,1)S(1)} %get-tuple-element.335), channel_id=1, source_target_pairs={{4,0},{8,4},{12,8},{16,12},{20,16},{24,20},{28,24},{0,28},{5,1},{9... | collective-permute-start | bytes 110600 | tf_op jit(solution)/shard_map/ppermute | solution.py:23
where the time goes:
time: 177 us; the launch traced here: 176 us
  waiting for transfers between devices  62.3 us (35%)
  local copies, waits for them, and re-layouts  37.2 us (21%)
  matrix products  31.5 us (18%)
  other arithmetic  24.5 us (14%)
  starting transfers between devices  16.7 us (9%)
  between operations  2.82 us (2%)
    all_to_all x1, waiting for transfers between devices, on_device(): lax.all_to_all(slot_back, ('elem', 'span'), split_axis=1, concat_axis=1,...  40.9 us
    dot_general x56, matrix products, conv_levels(): jnp.einsum('ok,kln->oln', flat_weight, stacked, preferred_element_type=jn...  31.5 us
    gather x3, other arithmetic, on_device(): within = block_ranks - offsets[source]  20.1 us
    all_to_all x1, waiting for transfers between devices, on_device(): lax.all_to_all(outgoing, ('elem', 'span'), split_axis=1, concat_axis=1, t...  19.6 us
    slice x56, local copies, waits for them, and re-layouts, conv_levels(): padded[:, tap_index:tap_index + levels, :]  12 us
    all_to_all x1, starting transfers between devices, on_device(): lax.all_to_all(outgoing, ('elem', 'span'), split_axis=1, concat_axis=1, t...  7.56 us
    scatter x1, local copies, waits for them, and re-layouts, on_device(): owned = owned.at[edge_local.reshape(-1)].set(merged.reshape(-1, feat_out))  3.86 us
    all_to_all x1, starting transfers between devices, on_device(): lax.all_to_all(slot_back, ('elem', 'span'), split_axis=1, concat_axis=1,...  3.83 us
  transfers between devices with their start and end apart: 6, of which 4 were waited for; matrix products, arithmetic and copies ran while one was open for 13% of the time, Pallas kernels for 0%

commit v1 on v0

--- a/solution.py
+++ b/solution.py
@@ -1,3 +1,4 @@
+import functools
 import math
 import jax
 import jax.numpy as jnp
@@ -9,6 +10,21 @@
 F_OUT = 16
 DEPTH = 8
 SPAN = 256
+
+
+def lay_spots_up(shard_in, net_axis, out_dim, along_dim):
+    return jnp.concatenate(
+        jax.lax.all_to_all(
+            jnp.stack(jnp.split(shard_in, jax.lax.axis_size(net_axis), out_dim), axis=0),
+            net_axis,
+            0,
+            0,
+        ),
+        along_dim,
+    )
+
+
+hold_row_up = functools.partial(lay_spots_up, net_axis=("elem", "span"), out_dim=1, along_dim=1)
 
 
 def extended(cells, sides, width):
@@ -116,7 +132,7 @@
         jnp.zeros((slot_count * devices, feat_out), jnp.bfloat16).at[flat_index].set(computed)
     )
     slot_back = slot_back.reshape(slot_count, devices, feat_out)
-    returned = lax.all_to_all(slot_back, ("elem", "span"), split_axis=1, concat_axis=1, tiled=True)
+    returned = hold_row_up(slot_back)
     owned = jnp.roll(returned, -rank_start, axis=1).reshape(col_max, feat_out)
     edge_local = edge_index[0]
     edge_rows = owned[edge_local]

time: 177 us -> 198 us (1.12)
  local copies, waits for them, and re-layouts: 37.2 us -> 58.5 us
    unnamed x20 -> x51, local copies, waits for them, and re-layouts: 0.05 us -> 19.6 us
    split x0 -> x2, local copies, waits for them, and re-layouts: none -> 2.88 us  [lay_spots_up(): jnp.split(shard_in, jax.lax.axis_size(net_axis), out_dim)]
  transfers between devices with their start and end apart: 6 -> 6, of which waited for: 4 -> 4; matrix products, arithmetic and copies ran while one was open for 13% -> 11% of each run, Pallas kernels for 0% -> 0%
where the time goes in v1:
time: 198 us
  waiting for transfers between devices  62.3 us (31%)
  local copies, waits for them, and re-layouts  58.5 us (30%)
  matrix products  31.5 us (16%)
  other arithmetic  24.5 us (12%)
  starting transfers between devices  16.7 us (8%)
  between operations  2.86 us (1%)
    all_to_all x1, waiting for transfers between devices, lay_spots_up(): jax.lax.all_to_all(jnp.stack(jnp.split(shard_in, jax.lax.axis_size(net_ax...  40.9 us
    dot_general x56, matrix products, conv_levels(): jnp.einsum('ok,kln->oln', flat_weight, stacked, preferred_element_type=jn...  31.5 us
    gather x3, other arithmetic, on_device(): within = block_ranks - offsets[source]  20.1 us
    all_to_all x1, waiting for transfers between devices, on_device(): lax.all_to_all(outgoing, ('elem', 'span'), split_axis=1, concat_axis=1, t...  19.6 us
    unnamed x51, local copies, waits for them, and re-layouts  19.6 us
    slice x56, local copies, waits for them, and re-layouts, conv_levels(): padded[:, tap_index:tap_index + levels, :]  12 us
    all_to_all x1, starting transfers between devices, on_device(): lax.all_to_all(outgoing, ('elem', 'span'), split_axis=1, concat_axis=1, t...  7.56 us
  transfers between devices with their start and end apart: 6, of which 4 were waited for; matrix products, arithmetic and copies ran while one was open for 11% of the time, Pallas kernels for 0%

profile of v1, /device:TPU:0, one launch (start us, length us, event | category | flops | bytes accessed | tf_op | source)
XLA Modules:
  0.0 197.6 jit_solution(8230490490805300454)
XLA Ops:
  0.0 0.7 copy.1201
  3.5 2.8 %fusion.332 = bf16[24,32,1152]{2,1,0:T(8,128)(2,1)S(1)} fusion(s32[]{:T(128)S(6)} %select_n.75, bf16[24,32,1152]{2,1,0:T(8,128)(2,1)} %bitcast.595), kind=kLoop, calls=%fused_computation.341 | loop fusion | flops 3538944 | bytes 3538948 | tf_op jit(solution)/shard_map/jit(_roll_dynamic)/concatenate | solution.py:119
  6.2 1.7 copy.1202
  8.0 7.6 %all-to-all-start = ((bf16[24,32,1152]{2,0,1:T(8,128)(2,1)}), bf16[24,32,1152]{2,0,1:T(8,128)(2,1)}, u32[]{:S(2)}, u32[]{:S(2)}) async-start(bf16[24,32,1152]{2,0,1:T(8,128)(2,1)} %copy.1202), calls=%async_computation | async-start | bytes 3538944 | tf_op jit(solution)/shard_map/all_to_all | solution.py:120
  16.8 0.7 fusion.352
  17.6 3.6 %compare_select_fusion.3 = (s32[256,1]{0,1:T(1,128)S(1)}, s32[256,1]{0,1:T(1,128)S(1)}) fusion(s32[]{:T(128)} %bitcast.132, s32[]{:T(128)} %bitcast.133, s32[]{:T(128)} %bitcast.134, s32[]{:T(128)} %bitcast.135, s32[]{:T(128)} %bitcast.136, s32[]{:T(128)} %bitcast.137, s32[256,1]{0,1:T(1,128)S(1)} %bitcast.607), kind=kLoop, calls=%fused_computation.429 | loop fusion | flops 3840 | bytes 3096 | tf_op jit(solution)/shard_map/gather | solution.py:123
  21.3 16.4 %select_select_fusion = s32[256]{0:T(256)S(1)} fusion(pred[256]{0:T(512)(128)(4,1)S(1)} %get-tuple-element.497, pred[256]{0:T(512)(128)(4,1)S(1)} %get-tuple-element.496, pred[256]{0:T(512)(128)(4,1)S(1)} %get-tuple-element.495, pred[256]{0:T(512)(128)(4,1)S(1)} %get-tuple-element.494, pred[256]{0:T(512)(128)(4,1)S(1)} %get-tuple-element.493, ...), kind=kLoop, calls=%fused_computation.440 | loop fusion | flops 6656 | bytes 8808 | tf_op jit(solution)/shard_map/gather | solution.py:123
  37.7 19.6 %all-to-all-done = bf16[24,32,1152]{2,0,1:T(8,128)(2,1)} async-done(((bf16[24,32,1152]{2,0,1:T(8,128)(2,1)}), bf16[24,32,1152]{2,0,1:T(8,128)(2,1)}, u32[]{:S(2)}, u32[]{:S(2)}) %all-to-all-start) | async-done | bytes 1769504 | tf_op jit(solution)/shard_map/all_to_all | solution.py:120
  57.3 1.7 copy.1203
  59.0 1.3 gather_fusion
  60.3 53.1 %while.12 = (s32[]{:T(128)}, bf16[2,128,1152]{2,1,0:T(8,128)(2,1)}, bf16[2,128,1152]{2,1,0:T(8,128)(2,1)S(1)}, bf16[3,32,16]{1,2,0:T(8,128)(2,1)S(1)}, bf16[8,3,...) while((s32[]{:T(128)}, bf16[2,128,1152]{2,1,0:T(8,128)(2,1)}, ...), condition=%wide.region_3.5_spmd, body=%wide.region_2.4_spmd.sunk | while | flops 2317344768 | bytes 136280240 | solution.py:127
  69.6 0.6 add_convert_fusion.56
  70.6 0.6 add_convert_fusion.57
  71.5 0.6 add_convert_fusion.58
  72.5 0.6 add_convert_fusion.59
  73.5 0.6 add_convert_fusion.60
  74.4 0.6 add_convert_fusion.61
  75.4 0.6 add_convert_fusion.62
  76.3 0.6 add_convert_fusion.63
  78.0 1.6 multiply_convert_fusion.11
  86.1 0.8 copy-done.9
  96.1 0.6 add_convert_fusion.56
  97.0 0.6 add_convert_fusion.57
  98.0 0.6 add_convert_fusion.58
  99.0 0.6 add_convert_fusion.59
  99.9 0.6 add_convert_fusion.60
  100.9 0.6 add_convert_fusion.61
  101.8 0.6 add_convert_fusion.62
  102.8 0.6 add_convert_fusion.63
  104.5 1.6 multiply_convert_fusion.11
  112.6 0.8 copy-done.9
  113.4 2.7 %scatter_custom_fusion = bf16[768,1152]{1,0:T(8,128)(2,1)S(1)} fusion(s32[256]{0:T(256)} %bitcast.610, bf16[256,1152]{1,0:T(8,128)(2,1)} %bitcast.614, bf16[]{:T(256)} %constant.112.clone.1), kind=kCustom, calls=%fused_computation.342 | custom fusion | bytes 1769984 | tf_op jit(solution)/shard_map/scatter | solution.py:132
  116.2 1.1 fusion.351
  117.3 1.7 fusion.350
  119.1 0.6 constant_dynamic-update-slice_fusion.32
  119.7 0.6 constant_dynamic-update-slice_fusion.31
  120.3 0.6 constant_dynamic-update-slice_fusion.30
  121.0 0.6 constant_dynamic-update-slice_fusion.29
  121.6 0.6 constant_dynamic-update-slice_fusion.28
  122.2 0.6 constant_dynamic-update-slice_fusion.27
  139.2 3.8 %all-to-all-start.1 = ((bf16[32,24,1,1152]{3,1,2,0:T(8,128)(2,1)}), bf16[32,24,1,1152]{3,1,2,0:T(8,128)(2,1)S(1)}, u32[]{:S(2)}, u32[]{:S(2)}) async-start(bf16[32,24,1,1152]{3,1,2,0:T(8,128)(2,1)} %constant_dynamic-update-slice_fusion.1), calls=%async_computation.1 | async-start | bytes 3538944 | tf_op jit(solution)/shard_map/all_to_all | solution.py:17
  143.9 40.9 %all-to-all-done.1 = bf16[32,24,1,1152]{3,1,2,0:T(8,128)(2,1)S(1)} async-done(((bf16[32,24,1,1152]{3,1,2,0:T(8,128)(2,1)}), bf16[32,24,1,1152]{3,1,2,0:T(8,128)(2,1)S(1)}, u32[]{:S(2)}, u32[]{:S(2)}) %all-to-all-start.1) | async-done | bytes 1769504 | tf_op jit(solution)/shard_map/all_to_all | solution.py:17
  184.8 0.7 fusion.331
  185.8 0.7 gather_fusion.1
  186.5 1.5 collective-permute-start
  188.5 3.3 %collective-permute-start.1 = (bf16[1,16,1152]{2,1,0:T(8,128)(2,1)S(1)}, bf16[1,16,1152]{2,1,0:T(8,128)(2,1)S(1)}, u32[]{:S(2)}, u32[]{:S(2)}) collective-permute-start(bf16[1,16,1152]{2,1,0:T(8,128)(2,1)S(1)} %get-tuple-element.647), channel_id=1, source_target_pairs={{4,0},{8,4},{12,8},{16,12},{20,16},{24,20},{28,24},{0,28},{5,1},{9... | collective-permute-start | bytes 110600 | tf_op jit(solution)/shard_map/ppermute | solution.py:39
  191.8 1.4 collective-permute-done
  193.7 3.9 %scatter_fusion = bf16[768,1152]{1,0:T(8,128)(2,1)} fusion(bf16[768,1152]{1,0:T(8,128)(2,1)} %bitcast.592, s32[64]{0:T(128)S(1)} %fusion.347, bf16[64,1152]{1,0:T(8,128)(2,1)S(1)} %bitcast.606), kind=kCustom, calls=%fused_computation.3 | custom fusion | bytes 442624 | tf_op jit(solution)/shard_map/scatter | solution.py:147
  (235 shorter events, 56.9 us)
Async XLA Ops:
  8.0 7.6 %copy-start.5 = (bf16[3,16,32]{2,1,0:T(8,128)(2,1)S(1)}, bf16[3,16,32]{2,1,0:T(8,128)(2,1)}, u32[]{:S(2)}) copy-start(bf16[3,16,32]{2,1,0:T(8,128)(2,1)} %param.23) | copy-start | bytes 9220
  8.0 7.6 %copy-start.4 = (bf16[3,32,96]{2,1,0:T(8,128)(2,1)S(1)}, bf16[3,32,96]{2,1,0:T(8,128)(2,1)}, u32[]{:S(2)}) copy-start(bf16[3,32,96]{2,1,0:T(8,128)(2,1)} %param.21) | copy-start | bytes 55300
  8.0 7.7 %copy-start.2 = (bf16[8,3,32,32]{3,2,1,0:T(8,128)(2,1)S(1)}, bf16[8,3,32,32]{3,2,1,0:T(8,128)(2,1)}, u32[]{:S(2)}) copy-start(bf16[8,3,32,32]{3,2,1,0:T(8,128)(2,1)} %param.18) | copy-start | bytes 147460
  8.0 7.8 %copy-start.3 = (bf16[8,3,32,32]{3,2,1,0:T(8,128)(2,1)S(1)}, bf16[8,3,32,32]{3,2,1,0:T(8,128)(2,1)}, u32[]{:S(2)}) copy-start(bf16[8,3,32,32]{3,2,1,0:T(8,128)(2,1)} %param.22) | copy-start | bytes 147460
  8.0 8.0 %copy-start.1 = (bf16[8,3,64,64]{3,2,1,0:T(8,128)(2,1)S(1)}, bf16[8,3,64,64]{3,2,1,0:T(8,128)(2,1)}, u32[]{:S(2)}) copy-start(bf16[8,3,64,64]{3,2,1,0:T(8,128)(2,1)} %param.20) | copy-start | bytes 589828
  8.0 49.3 %all-to-all-start = ((bf16[24,32,1152]{2,0,1:T(8,128)(2,1)}), bf16[24,32,1152]{2,0,1:T(8,128)(2,1)}, u32[]{:S(2)}, u32[]{:S(2)}) async-start(bf16[24,32,1152]{2,0,1:T(8,128)(2,1)} %copy.1202), calls=%async_computation | async-start | bytes 3538944 | tf_op jit(solution)/shard_map/all_to_all | solution.py:120
  37.7 21.3 %copy-start.7 = (s32[256,1]{0,1:T(1,128)}, s32[256,1]{0,1:T(1,128)S(1)}, u32[]{:S(2)}) copy-start(s32[256,1]{0,1:T(1,128)S(1)} %compare_select_fusion) | copy-start | bytes 3076
  59.0 1.3 copy-start.10
  59.0 1.3 copy-start.11
  85.0 1.1 copy-start.8
  86.1 0.8 copy-start.9
  111.5 1.1 copy-start.8
  112.6 0.8 copy-start.9
  139.2 4.5 %copy-start.6 = (s32[1,4,16]{2,1,0:T(4,128)S(1)}, s32[1,4,16]{2,1,0:T(4,128)}, u32[]{:S(2)}) copy-start(s32[1,4,16]{2,1,0:T(4,128)} %param.16) | copy-start | bytes 772
  139.2 45.6 %all-to-all-start.1 = ((bf16[32,24,1,1152]{3,1,2,0:T(8,128)(2,1)}), bf16[32,24,1,1152]{3,1,2,0:T(8,128)(2,1)S(1)}, u32[]{:S(2)}, u32[]{:S(2)}) async-start(bf16[32,24,1,1152]{3,1,2,0:T(8,128)(2,1)} %constant_dynamic-update-slice_fusion.1), calls=%async_computation.1 | async-start | bytes 3538944 | tf_op jit(solution)/shard_map/all_to_all | solution.py:17
  185.7 7.9 %copy-start = (bf16[24,32,1152]{2,1,0:T(8,128)(2,1)}, bf16[24,32,1152]{2,1,0:T(8,128)(2,1)S(1)}, u32[]{:S(2)}) copy-start(bf16[24,32,1152]{2,1,0:T(8,128)(2,1)S(1)} %copy.1211) | copy-start | bytes 5308420
  186.5 6.7 %collective-permute-start = (bf16[1,16,1152]{2,1,0:T(8,128)(2,1)S(1)}, bf16[1,16,1152]{2,1,0:T(8,128)(2,1)S(1)}, u32[]{:S(2)}, u32[]{:S(2)}) collective-permute-start(bf16[1,16,1152]{2,1,0:T(8,128)(2,1)S(1)} %get-tuple-element.644), channel_id=1, source_target_pairs={{0,4},{4,8},{8,12},{12,16},{16,20},{20,24},{24,28},{28,0},{1,5},{5... | collective-permute-start | bytes 110600 | tf_op jit(solution)/shard_map/ppermute | solution.py:37
  188.0 5.3 %collective-permute-start.3 = (bf16[1,16,1152]{2,1,0:T(8,128)(2,1)S(1)}, bf16[1,16,1152]{2,1,0:T(8,128)(2,1)S(1)}, u32[]{:S(2)}, u32[]{:S(2)}) collective-permute-start(bf16[1,16,1152]{2,1,0:T(8,128)(2,1)S(1)} %get-tuple-element.645), channel_id=1, source_target_pairs={{1,0},{2,1},{3,2},{0,3},{5,4},{6,5},{7,6},{4,7},{9,8},{10,9},{11,1... | collective-permute-start | bytes 110600 | tf_op jit(solution)/shard_map/ppermute | solution.py:39
  188.5 4.8 %collective-permute-start.2 = (bf16[1,16,1152]{2,1,0:T(8,128)(2,1)S(1)}, bf16[1,16,1152]{2,1,0:T(8,128)(2,1)S(1)}, u32[]{:S(2)}, u32[]{:S(2)}) collective-permute-start(bf16[1,16,1152]{2,1,0:T(8,128)(2,1)S(1)} %get-tuple-element.646), channel_id=1, source_target_pairs={{0,1},{1,2},{2,3},{3,0},{4,5},{5,6},{6,7},{7,4},{8,9},{9,10},{10,1... | collective-permute-start | bytes 110600 | tf_op jit(solution)/shard_map/ppermute | solution.py:37
  188.5 5.1 %collective-permute-start.1 = (bf16[1,16,1152]{2,1,0:T(8,128)(2,1)S(1)}, bf16[1,16,1152]{2,1,0:T(8,128)(2,1)S(1)}, u32[]{:S(2)}, u32[]{:S(2)}) collective-permute-start(bf16[1,16,1152]{2,1,0:T(8,128)(2,1)S(1)} %get-tuple-element.647), channel_id=1, source_target_pairs={{4,0},{8,4},{12,8},{16,12},{20,16},{24,20},{28,24},{0,28},{5,1},{9... | collective-permute-start | bytes 110600 | tf_op jit(solution)/shard_map/ppermute | solution.py:39
